TPU v7x, 32 devices: a whole 2x2x4 slice. The times are simulated.
32 devices in a mesh: dp: 8 (over z, core), tensor: 4 (over y, x).
Axes of the slice: x: 2, y: 2, z: 4, core: 2. Of those that a mesh axis runs over, the one named last changes fastest.
Arguments:
- inputs: bfloat16 [49152, 512], P(('dp', 'tensor')), may hold values from -6 to 6
- w_qkv: bfloat16 [2, 3, 512, 512], P(None, None, 'dp', 'tensor'), may hold values from -0.25 to 0.25
- w_out: bfloat16 [2, 512, 512], P(None, 'tensor', 'dp'), may hold values from -0.75 to 0.75
- w_up: bfloat16 [2, 512, 2048], P(None, 'dp', 'tensor'), may hold values from -0.25 to 0.25
- w_down: bfloat16 [2, 2048, 512], P(None, 'tensor', 'dp'), may hold values from -0.125 to 0.125
- ln_gain: float32 [2, 2, 512], replicated, may hold values from 0.5 to 1.5
- ln_bias: float32 [2, 2, 512], replicated, may hold values from -3 to 3
- bias_qv: float32 [2, 2, 512], P(None, None, 'tensor'), may hold values from -3 to 3
- bias_up: float32 [2, 2048], P(None, 'tensor'), may hold values from -3 to 3
- branch_bias: float32 [2, 2, 512], replicated, may hold values from -3 to 3
- cotangent: float32 [49152, 512], P(('dp', 'tensor')), may hold values from -6 to 6
Outputs:
- outputs: bfloat16 [49152, 512], P(('dp', 'tensor'))
- input_grad: float32 [49152, 512], P(('dp', 'tensor'))
- grad_qkv: float32 [2, 3, 512, 512], P(None, None, 'dp', 'tensor')
- grad_out: float32 [2, 512, 512], P(None, 'tensor', 'dp')
- grad_up: float32 [2, 512, 2048], P(None, 'dp', 'tensor')
- grad_down: float32 [2, 2048, 512], P(None, 'tensor', 'dp')
- grad_ln_gain: float32 [2, 2, 512], replicated
- grad_ln_bias: float32 [2, 2, 512], replicated
- grad_bias_qv: float32 [2, 2, 512], P(None, None, 'tensor')
- grad_bias_up: float32 [2, 2048], P(None, 'tensor')
- grad_branch_bias: float32 [2, 2, 512], replicated
All inputs are finite; a program needn't handle non-finite values.
Results may differ from a plain program's by a relative error of at most 0.025.
Values may be sent and summed in bfloat16 or wider, within the bound.
A program may use at most 320 MiB of HBM per device.

v0:
```python
import math
import jax
import jax.numpy as jnp
from jax import lax
from jax.sharding import PartitionSpec as P

HD = 64
SPAN = 128
LEN = 2048
LAYERS = 2
highest = lax.Precision.HIGHEST
epsilon = 1e-05
masked_score = -1e30


def normalize(rows, gain, shift):
    centre = rows - jnp.mean(rows, -1, keepdims=True)
    spread = jnp.mean(centre * centre, -1, keepdims=True)
    return centre * lax.rsqrt(spread + epsilon) * gain + shift


def gelu_exact(values):
    return jax.nn.gelu(values, approximate=False)


def to_heads(rows):
    return rows.reshape(-1, LEN // SPAN, SPAN, rows.shape[1] // HD, HD)


def score_blocks(head_queries, head_keys, key_mean):
    scale = HD ** (-0.5)
    blocks = LEN // SPAN
    direct = (
        jnp.einsum(
            "gbihe,gbjhe->gbhij", head_queries, head_keys, preferred_element_type=jnp.float32
        )
        * scale
    )
    summary = jnp.einsum(
        "gbihe,gche->gbhic", head_queries.astype(jnp.float32), key_mean, precision=highest
    ) * scale + math.log(SPAN)
    inside = lax.broadcasted_iota(jnp.int32, (SPAN, SPAN), 0) >= lax.broadcasted_iota(
        jnp.int32, (SPAN, SPAN), 1
    )
    earlier = lax.broadcasted_iota(jnp.int32, (blocks, 1, 1, blocks), 0) > lax.broadcasted_iota(
        jnp.int32, (blocks, 1, 1, blocks), 3
    )
    return (jnp.where(inside, direct, masked_score), jnp.where(earlier, summary, masked_score))


def attend(query_rows, key_rows, value_rows):
    head_queries, head_keys, head_values = (
        to_heads(query_rows),
        to_heads(key_rows),
        to_heads(value_rows),
    )
    key_mean = jnp.mean(head_keys.astype(jnp.float32), 2)
    value_mean = jnp.mean(head_values.astype(jnp.float32), 2)
    direct, summary = score_blocks(head_queries, head_keys, key_mean)
    top = jnp.maximum(jnp.max(direct, -1), jnp.max(summary, -1))[..., None]
    direct_weight = jnp.exp(direct - top)
    summary_weight = jnp.exp(summary - top)
    total = jnp.sum(direct_weight, -1, keepdims=True) + jnp.sum(summary_weight, -1, keepdims=True)
    direct_prob = direct_weight / total
    summary_prob = summary_weight / total
    mixed = jnp.einsum(
        "gbhij,gbjhe->gbihe",
        direct_prob.astype(jnp.bfloat16),
        head_values,
        preferred_element_type=jnp.float32,
    )
    mixed = mixed + jnp.einsum("gbhic,gche->gbihe", summary_prob, value_mean, precision=highest)
    log_total = (top + jnp.log(total))[..., 0]
    return (mixed.reshape(query_rows.shape), log_total)


def attend_back(query_rows, key_rows, value_rows, log_total, grad_rows):
    scale = HD ** (-0.5)
    head_queries, head_keys, head_values = (
        to_heads(query_rows),
        to_heads(key_rows),
        to_heads(value_rows),
    )
    head_grads = to_heads(grad_rows)
    key_mean = jnp.mean(head_keys.astype(jnp.float32), 2)
    value_mean = jnp.mean(head_values.astype(jnp.float32), 2)
    direct, summary = score_blocks(head_queries, head_keys, key_mean)
    direct_prob = jnp.exp(direct - log_total[..., None])
    summary_prob = jnp.exp(summary - log_total[..., None])
    grad_float = head_grads.astype(jnp.float32)
    query_float = head_queries.astype(jnp.float32)
    direct_grad = jnp.einsum(
        "gbihe,gbjhe->gbhij", head_grads, head_values, preferred_element_type=jnp.float32
    )
    summary_grad = jnp.einsum("gbihe,gche->gbhic", grad_float, value_mean, precision=highest)
    centre = jnp.sum(direct_prob * direct_grad, -1, keepdims=True) + jnp.sum(
        summary_prob * summary_grad, -1, keepdims=True
    )
    direct_score = (direct_prob * (direct_grad - centre)).astype(jnp.bfloat16)
    summary_score = summary_prob * (summary_grad - centre)
    grad_query = jnp.einsum(
        "gbhij,gbjhe->gbihe", direct_score, head_keys, preferred_element_type=jnp.float32
    )
    grad_query = (
        grad_query + jnp.einsum("gbhic,gche->gbihe", summary_score, key_mean, precision=highest)
    ) * scale
    key_block = jnp.einsum("gbhic,gbihe->gche", summary_score, query_float, precision=highest) * (
        scale / SPAN
    )
    grad_key = (
        jnp.einsum(
            "gbhij,gbihe->gbjhe", direct_score, head_queries, preferred_element_type=jnp.float32
        )
        * scale
        + key_block[:, :, None]
    )
    value_block = (
        jnp.einsum("gbhic,gbihe->gche", summary_prob, grad_float, precision=highest) / SPAN
    )
    grad_value = (
        jnp.einsum(
            "gbhij,gbihe->gbjhe",
            direct_prob.astype(jnp.bfloat16),
            head_grads,
            preferred_element_type=jnp.float32,
        )
        + value_block[:, :, None]
    )
    shape = query_rows.shape
    return (grad_query.reshape(shape), grad_key.reshape(shape), grad_value.reshape(shape))


def fetch(first, second, third, fourth):
    return (
        lax.all_gather(first, "dp", axis=2, tiled=True),
        lax.all_gather(second, "dp", axis=2, tiled=True),
        lax.all_gather(third, "dp", axis=1, tiled=True),
        lax.all_gather(fourth, "dp", axis=2, tiled=True),
    )


def return_grads(first, second, third, fourth):
    return (
        lax.psum_scatter(first.astype(jnp.bfloat16), "dp", scatter_dimension=2, tiled=True).astype(
            jnp.float32
        ),
        lax.psum_scatter(second.astype(jnp.bfloat16), "dp", scatter_dimension=2, tiled=True).astype(
            jnp.float32
        ),
        lax.psum_scatter(third.astype(jnp.bfloat16), "dp", scatter_dimension=1, tiled=True).astype(
            jnp.float32
        ),
        lax.psum_scatter(fourth.astype(jnp.bfloat16), "dp", scatter_dimension=2, tiled=True).astype(
            jnp.float32
        ),
    )


def layer_weights(w_qkv, w_out, w_up, w_down, layer):
    gathered = fetch(
        w_qkv[layer : layer + 1],
        w_out[layer : layer + 1],
        w_up[layer : layer + 1],
        w_down[layer : layer + 1],
    )
    return tuple((part[0] for part in gathered))


def spread_only(rows, project):
    return project(lax.all_gather(rows, "tensor", axis=0, tiled=True))


def fold_again(rows, grads):
    return jnp.einsum(
        "td,tc->dc",
        lax.all_gather(rows, "tensor", axis=0, tiled=True),
        grads,
        preferred_element_type=jnp.float32,
    )


def spread_grads(rows, project):
    piece = lax.all_gather(rows, "tensor", axis=0, tiled=True)
    return (piece, project(piece))


def slice_term(source, weight, form):
    return jnp.einsum(form, source, weight, preferred_element_type=jnp.float32)


def rows_sum(source, weight, form):
    return lax.psum_scatter(
        slice_term(source, weight, form).astype(jnp.bfloat16),
        "tensor",
        scatter_dimension=0,
        tiled=True,
    ).astype(jnp.float32)


def grads_sum(source, weight, form):
    return lax.psum_scatter(
        slice_term(source, weight, form).astype(jnp.bfloat16),
        "tensor",
        scatter_dimension=0,
        tiled=True,
    ).astype(jnp.float32)


def group_rows(token_att, out_whole):
    groups = lax.axis_size("tensor")
    parts = token_att.reshape(token_att.shape[0], groups, -1)
    grouped = out_whole.reshape(groups, -1, out_whole.shape[1])
    partial_value = jnp.einsum("tgc,gcd->tgd", parts, grouped, preferred_element_type=jnp.float32)
    return jnp.sum(partial_value.astype(jnp.bfloat16), 1, dtype=jnp.float32)


def group_grads(token_grads, qkv_whole):
    groups = lax.axis_size("tensor")
    parts = token_grads.reshape(token_grads.shape[0], 3, groups, -1)
    grouped = qkv_whole.reshape(3, qkv_whole.shape[1], groups, -1)
    partial_value = jnp.einsum("tsgc,sdgc->tgd", parts, grouped, preferred_element_type=jnp.float32)
    return jnp.sum(partial_value.astype(jnp.bfloat16), 1, dtype=jnp.float32)


def forward_layer(residual, matrices, gains, shifts, bias_pair, bias_hidden, branch_pair):
    w_qkv, w_out, w_up, w_down = matrices
    attn_in = normalize(residual, gains[0], shifts[0]).astype(jnp.bfloat16)

    def project_qkv(piece):
        return jnp.einsum("td,sdc->tsc", piece, w_qkv, preferred_element_type=jnp.float32)

    def project_up(piece):
        return jnp.dot(piece, w_up, preferred_element_type=jnp.float32)

    mixed_qkv = spread_only(attn_in, project_qkv)
    queries = (mixed_qkv[:, 0] + bias_pair[0]).astype(jnp.bfloat16)
    keys_now = mixed_qkv[:, 1].astype(jnp.bfloat16)
    values_now = (mixed_qkv[:, 2] + bias_pair[1]).astype(jnp.bfloat16)
    mixed, log_total = attend(queries, keys_now, values_now)
    attended = mixed.astype(jnp.bfloat16)
    qkv_whole, out_whole = (
        lax.all_gather(w_qkv, "tensor", axis=2, tiled=True),
        lax.all_gather(w_out, "tensor", axis=0, tiled=True),
    )
    token_att = lax.all_to_all(attended, "tensor", split_axis=0, concat_axis=1, tiled=True)
    attn_branch = group_rows(token_att, out_whole)
    middle = residual + attn_branch + branch_pair[0]
    mlp_in = normalize(middle, gains[1], shifts[1]).astype(jnp.bfloat16)
    raised = spread_only(mlp_in, project_up)
    hidden = raised + bias_hidden
    activated = gelu_exact(hidden).astype(jnp.bfloat16)
    result = middle + rows_sum(activated, w_down, "tc,cd->td") + branch_pair[1]
    saved = (
        residual,
        middle,
        attn_in,
        mlp_in,
        None,
        None,
        queries,
        keys_now,
        values_now,
        log_total,
        attended,
        hidden,
        activated,
        qkv_whole,
    )
    return (result, saved)


def backward_layer(grad_residual, saved, matrices, gains, shifts):
    w_qkv, w_out, w_up, w_down = matrices
    (
        residual,
        middle,
        attn_in,
        mlp_in,
        attn_rows,
        mlp_rows,
        queries,
        keys_now,
        values_now,
        log_total,
        attended,
        hidden,
        activated,
        qkv_whole,
    ) = saved
    down_bias_grad = jnp.sum(grad_residual, 0)

    def back_down(piece):
        return jnp.einsum("td,fd->tf", piece, w_down, preferred_element_type=jnp.float32)

    gathered_out, grad_act = spread_grads(grad_residual.astype(jnp.bfloat16), back_down)
    down_grad = jnp.einsum("tf,td->fd", activated, gathered_out, preferred_element_type=jnp.float32)
    grad_hidden = jax.vjp(gelu_exact, hidden)[1](grad_act)[0].astype(jnp.bfloat16)
    up_bias_grad = jnp.sum(grad_hidden, 0, dtype=jnp.float32)
    up_grad = fold_again(mlp_in, grad_hidden)
    grad_mlp_in = grads_sum(grad_hidden, w_up, "tf,df->td")
    norm_back = jax.vjp(normalize, middle, gains[1], shifts[1])[1]
    grad_norm, gain_second, shift_second = norm_back(grad_mlp_in)
    grad_middle = grad_residual + grad_norm
    attn_bias_grad = jnp.sum(grad_middle, 0)

    def back_out(piece):
        return jnp.einsum("td,cd->tc", piece, w_out, preferred_element_type=jnp.float32)

    gathered_mid, grad_attended = spread_grads(grad_middle.astype(jnp.bfloat16), back_out)
    out_grad = jnp.einsum("tc,td->cd", attended, gathered_mid, preferred_element_type=jnp.float32)
    grad_query, grad_key, grad_value = attend_back(
        queries, keys_now, values_now, log_total, grad_attended.astype(jnp.bfloat16)
    )
    grad_query = grad_query.astype(jnp.bfloat16)
    grad_key = grad_key.astype(jnp.bfloat16)
    grad_value = grad_value.astype(jnp.bfloat16)
    pair_grad = jnp.stack(
        [jnp.sum(grad_query, 0, dtype=jnp.float32), jnp.sum(grad_value, 0, dtype=jnp.float32)]
    )
    stacked = jnp.stack([grad_query, grad_key, grad_value], 1)
    flat_grad = fold_again(attn_in, stacked.reshape(stacked.shape[0], -1))
    qkv_grad = jnp.transpose(flat_grad.reshape(flat_grad.shape[0], 3, -1), (1, 0, 2))
    token_grads = lax.all_to_all(stacked, "tensor", split_axis=0, concat_axis=2, tiled=True)
    grad_attn_in = group_grads(token_grads, qkv_whole)
    first_back = jax.vjp(normalize, residual, gains[0], shifts[0])[1]
    grad_first, gain_first, shift_first = first_back(grad_attn_in)
    grad_input = grad_middle + grad_first
    matrix_part = (qkv_grad[None], out_grad[None], up_grad[None], down_grad[None])
    shared_part = (
        jnp.stack([gain_first, gain_second]),
        jnp.stack([shift_first, shift_second]),
        jnp.stack([attn_bias_grad, down_bias_grad]),
    )
    head_part = (pair_grad, up_bias_grad)
    return (grad_input, matrix_part, shared_part, head_part)


def body(
    inputs, w_qkv, w_out, w_up, w_down, ln_gain, ln_bias, bias_qv, bias_up, branch_bias, cotangent
):
    residual = inputs.astype(jnp.float32)
    saved_all = []
    for layer in range(LAYERS):
        matrices = layer_weights(w_qkv, w_out, w_up, w_down, layer)
        residual, saved = forward_layer(
            residual,
            matrices,
            ln_gain[layer],
            ln_bias[layer],
            bias_qv[layer],
            bias_up[layer],
            branch_bias[layer],
        )
        saved_all.append(saved)
    outputs = residual.astype(jnp.bfloat16)
    grad_residual = cotangent
    matrix_grads = [None] * LAYERS
    shared_grads = [None] * LAYERS
    head_grads = [None] * LAYERS
    for layer in reversed(range(LAYERS)):
        matrices = layer_weights(w_qkv, w_out, w_up, w_down, layer)
        grad_residual, matrix_part, shared_part, head_part = backward_layer(
            grad_residual, saved_all[layer], matrices, ln_gain[layer], ln_bias[layer]
        )
        matrix_grads[layer] = return_grads(
            matrix_part[0], matrix_part[1], matrix_part[2], matrix_part[3]
        )
        shared_grads[layer] = shared_part
        head_grads[layer] = head_part
    joined = [jnp.concatenate([grads[index] for grads in matrix_grads], 0) for index in range(4)]
    gain_total = jnp.stack([grads[0] for grads in shared_grads])
    shift_total = jnp.stack([grads[1] for grads in shared_grads])
    branch_total = jnp.stack([grads[2] for grads in shared_grads])
    gain_sum, shift_sum, branch_sum = lax.psum(
        (gain_total, shift_total, branch_total), ("dp", "tensor")
    )
    pair_total = jnp.stack([grads[0] for grads in head_grads])
    hidden_total = jnp.stack([grads[1] for grads in head_grads])
    pair_sum, hidden_sum = lax.psum((pair_total, hidden_total), "dp")
    return (
        outputs,
        grad_residual,
        joined[0],
        joined[1],
        joined[2],
        joined[3],
        gain_sum,
        shift_sum,
        pair_sum,
        hidden_sum,
        branch_sum,
    )


def solution(mesh):
    return jax.shard_map(
        body,
        mesh=mesh,
        in_specs=(
            P(("dp", "tensor"), None),
            P(None, None, "dp", "tensor"),
            P(None, "tensor", "dp"),
            P(None, "dp", "tensor"),
            P(None, "tensor", "dp"),
            P(),
            P(),
            P(None, None, "tensor"),
            P(None, "tensor"),
            P(),
            P(("dp", "tensor"), None),
        ),
        out_specs=(
            P(("dp", "tensor"), None),
            P(("dp", "tensor"), None),
            P(None, None, "dp", "tensor"),
            P(None, "tensor", "dp"),
            P(None, "dp", "tensor"),
            P(None, "tensor", "dp"),
            P(),
            P(),
            P(None, None, "tensor"),
            P(None, "tensor"),
            P(),
        ),
        check_vma=False,
    )
```

profile of v0, /device:TPU:12, one launch (start us, length us, event | category | flops | bytes accessed | tf_op | source)
XLA Modules:
  0.0 1674.3 jit_solution(17339127591960681586)
XLA Ops:
  16.2 14.7 all_gather.71
  31.0 55.3 %all-gather.15.cloned.1.call-done = bf16[6144,512]{1,0:T(8,128)(2,1)} async-done(((bf16[1536,512]{1,0:T(8,128)(2,1)}), bf16[6144,512]{1,0:T(8,128)(2,1)}) %all-gather.15.cloned.1.call-update) | async-done | bytes 6291472 | tf_op jit(solution)/shard_map/all_gather | solution.py:170
  86.3 5.5 fusion.18
  127.3 5.7 copy.448
  132.9 6.3 reshape.482
  144.1 14.0 all_gather.72
  158.7 10.3 all-gather
  178.9 15.7 all_gather.75
  194.6 16.1 all_gather.76
  210.7 36.6 %all-gather.17.cloned.1.call-done = bf16[6144,512]{1,0:T(8,128)(2,1)} async-done(((bf16[1536,512]{1,0:T(8,128)(2,1)}), bf16[6144,512]{1,0:T(8,128)(2,1)}) %all-gather.17.cloned.1.call-update) | async-done | bytes 6291472 | tf_op jit(solution)/shard_map/all_gather | solution.py:170
  247.2 33.3 %multiply_convert_fusion.1 = (bf16[6144,512]{1,0:T(8,128)(2,1)S(1)}, f32[6144,512]{1,0:T(8,128)}, f32[6144,512]{1,0:T(8,128)}) fusion(f32[512]{0:T(512)S(1)} %bitcast.514, bf16[6144,512]{1,0:T(8,128)(2,1)} %all-gather.17.cloned.1.call-done, bf16[1,512,512]{2,1,0:T(8,128)(2,1)} %all_gather.75), kind=kOutput, calls=%fused_computation.28 | convolution fusion | flops 3428843520 | bytes 38275072 | tf_op jit(solution)/shard_map/dot_general | solution.py:233
  283.3 5.4 convolution_convert_fusion.3
  288.7 70.2 %reduce-scatter.21.cloned.1.call-done = bf16[1536,512]{1,0:T(8,128)(2,1)} async-done(((bf16[6144,512]{1,0:T(8,128)(2,1)}), bf16[1536,512]{1,0:T(8,128)(2,1)}) %reduce-scatter.21.cloned.1.call-update) | async-done | bytes 1572880 | tf_op jit(solution)/shard_map/reduce_scatter | solution.py:192
  364.4 14.9 all_gather.78
  379.3 55.4 %all-gather.19.cloned.1.call-done = bf16[6144,512]{1,0:T(8,128)(2,1)} async-done(((bf16[1536,512]{1,0:T(8,128)(2,1)}), bf16[6144,512]{1,0:T(8,128)(2,1)}) %all-gather.19.cloned.1.call-update) | async-done | bytes 6291472 | tf_op jit(solution)/shard_map/all_gather | solution.py:170
  434.7 5.5 fusion.14
  475.7 5.7 copy.449
  481.4 6.3 reshape.483
  487.7 4.9 all-to-all-start.1
  492.5 14.0 all_gather.79
  507.2 10.9 all-gather.1
  530.8 15.2 all_gather.82
  545.9 15.1 all_gather.83
  561.1 37.8 %all-gather.21.cloned.1.call-done = bf16[6144,512]{1,0:T(8,128)(2,1)} async-done(((bf16[1536,512]{1,0:T(8,128)(2,1)}), bf16[6144,512]{1,0:T(8,128)(2,1)}) %all-gather.21.cloned.1.call-update) | async-done | bytes 6291472 | tf_op jit(solution)/shard_map/all_gather | solution.py:170
  598.8 33.1 %multiply_convert_fusion = (bf16[6144,512]{1,0:T(8,128)(2,1)}, f32[6144,512]{1,0:T(8,128)}, f32[6144,512]{1,0:T(8,128)}) fusion(f32[512]{0:T(512)S(1)} %bitcast.517, bf16[6144,512]{1,0:T(8,128)(2,1)} %all-gather.21.cloned.1.call-done, bf16[1,512,512]{2,1,0:T(8,128)(2,1)S(1)} %all_gather.82), kind=kOutput, calls=%fused_computation.14 | convolution fusion | flops 3428843520 | bytes 38275072 | tf_op jit(solution)/shard_map/dot_general | solution.py:233
  631.9 38.8 %all-gather.23.cloned.1.call-done = bf16[6144,512]{1,0:T(8,128)(2,1)} async-done(((bf16[1536,512]{1,0:T(8,128)(2,1)}), bf16[6144,512]{1,0:T(8,128)(2,1)}) %all-gather.23.cloned.1.call-update) | async-done | bytes 6291472 | tf_op jit(solution)/shard_map/all_gather | solution.py:183
  670.7 14.1 convert_reduce_fusion.4
  687.5 5.4 convolution_convert_fusion.1
  693.0 8.3 convolution_convert_fusion.2
  701.7 61.4 %reduce-scatter.25.cloned.1.call-done = bf16[1536,512]{1,0:T(8,128)(2,1)} async-done(((bf16[6144,512]{1,0:T(8,128)(2,1)}), bf16[1536,512]{1,0:T(8,128)(2,1)}) %reduce-scatter.25.cloned.1.call-update) | async-done | bytes 1572880 | tf_op jit(solution)/shard_map/reduce_scatter | solution.py:201
  768.9 67.4 %reduce-scatter.23.cloned.1.call-done = bf16[1536,512]{1,0:T(8,128)(2,1)} async-done(((bf16[6144,512]{1,0:T(8,128)(2,1)}), bf16[1536,512]{1,0:T(8,128)(2,1)}) %reduce-scatter.23.cloned.1.call-update) | async-done | bytes 1572880 | tf_op jit(solution)/shard_map/reduce_scatter | solution.py:192
  836.3 5.1 fusion.269
  844.5 70.4 %all-gather.25.cloned.1.call-done = bf16[6144,512]{1,0:T(8,128)(2,1)} async-done(((bf16[1536,512]{1,0:T(8,128)(2,1)}), bf16[6144,512]{1,0:T(8,128)(2,1)}) %all-gather.25.cloned.1.call-update) | async-done | bytes 6291472 | tf_op jit(solution)/shard_map/all_gather | solution.py:183
  915.0 5.8 convolution_convert_fusion.5
  928.7 4.6 multiply_reduce_fusion.1
  945.5 6.5 multiply_convert_fusion.3
  962.9 5.2 convert_reduce_fusion.12
  976.1 10.1 copy.393
  986.2 5.8 all-to-all-start.2
  992.6 68.5 %all-gather.31.cloned.1.call-done = bf16[1,3,512,512]{3,2,1,0:T(8,128)(2,1)} async-done(((bf16[1,3,512,128]{3,2,1,0:T(8,128)(2,1)}), bf16[1,3,512,512]{3,2,1,0:T(8,128)(2,1)}) %all-gather.31.cloned.1.call-update) | async-done | bytes 1572880 | tf_op jit(solution)/shard_map/all_gather | solution.py:242
  1063.7 10.6 all-to-all-done.2
  1077.8 5.1 convert_reduce_fusion.2
  1090.3 72.9 %all-gather.27.cloned.1.call-done = bf16[6144,512]{1,0:T(8,128)(2,1)} async-done(((bf16[1536,512]{1,0:T(8,128)(2,1)}), bf16[6144,512]{1,0:T(8,128)(2,1)}) %all-gather.27.cloned.1.call-update) | async-done | bytes 6291472 | tf_op jit(solution)/shard_map/all_gather | solution.py:183
  1163.2 13.4 convert_reduce_fusion.5
  1179.3 5.3 convolution_convert_fusion
  1185.8 8.8 fusion.149
  1200.9 54.0 %reduce-scatter.27.cloned.1.call-done = bf16[1536,512]{1,0:T(8,128)(2,1)} async-done(((bf16[6144,512]{1,0:T(8,128)(2,1)}), bf16[1536,512]{1,0:T(8,128)(2,1)}) %reduce-scatter.27.cloned.1.call-update) | async-done | bytes 1572880 | tf_op jit(solution)/shard_map/reduce_scatter | solution.py:201
  1271.3 8.0 fusion.148
  1281.5 6.2 all-gather.33.cloned.1.call-done
  1293.9 8.9 fusion.147
  1302.8 14.4 reduce-scatter.43.cloned.1.call-done
  1318.3 8.9 fusion.146
  1327.2 63.8 %all-gather.29.cloned.1.call-done = bf16[6144,512]{1,0:T(8,128)(2,1)} async-done(((bf16[1536,512]{1,0:T(8,128)(2,1)}), bf16[6144,512]{1,0:T(8,128)(2,1)}) %all-gather.29.cloned.1.call-update) | async-done | bytes 6291472 | tf_op jit(solution)/shard_map/all_gather | solution.py:183
  1391.1 5.7 convolution_convert_fusion.4
  1444.5 10.2 copy.417
  1454.7 5.9 all-to-all-start.3
  1465.4 7.7 fusion.150
  1476.4 7.7 fusion.155
  1484.2 30.2 %reduce-scatter.33.cloned.1.call-done = bf16[1,64,512]{2,1,0:T(8,128)(2,1)} async-done(((bf16[1,512,512]{2,1,0:T(8,128)(2,1)}), bf16[1,64,512]{2,1,0:T(8,128)(2,1)}) %reduce-scatter.33.cloned.1.call-update) | async-done | bytes 65552 | tf_op jit(solution)/shard_map/reduce_scatter | solution.py:150
  1516.2 14.9 all-reduce.1
  1531.1 13.9 reduce-scatter.37.cloned.1.call-done
  1546.6 29.4 %reduce-scatter.31.cloned.1.call-done = bf16[1,3,64,128]{3,2,1,0:T(8,128)(2,1)} async-done(((bf16[1,3,512,128]{3,2,1,0:T(8,128)(2,1)}), bf16[1,3,64,128]{3,2,1,0:T(8,128)(2,1)}) %reduce-scatter.31.cloned.1.call-update) | async-done | bytes 49168 | tf_op jit(solution)/shard_map/reduce_scatter | solution.py:144
  1576.0 31.2 %reduce-scatter.29.cloned.1.call-done = bf16[1,3,64,128]{3,2,1,0:T(8,128)(2,1)} async-done(((bf16[1,3,512,128]{3,2,1,0:T(8,128)(2,1)}), bf16[1,3,64,128]{3,2,1,0:T(8,128)(2,1)}) %reduce-scatter.29.cloned.1.call-update) | async-done | bytes 49168 | tf_op jit(solution)/shard_map/reduce_scatter | solution.py:144
  1622.8 44.5 %all-reduce = (f32[2,2,512]{2,1,0:T(2,128)}, f32[2,2,512]{2,1,0:T(2,128)}, f32[2,2,512]{2,1,0:T(2,128)}) all-reduce(f32[2,2,512]{2,1,0:T(2,128)S(1)} %pad_maximum_fusion, f32[2,2,512]{2,1,0:T(2,128)S(1)} %pad_maximum_fusion.1, f32[2,2,512]{2,1,0:T(2,128)S(1)} %pad_maximum_fusion.2), channel_id=1, replica_groups=mesh['dp'=8,'tensor'=4] {'dp','tensor'}, use_global_device_ids=true, to_apply=%region_52.53 | all-reduce | flops 6144 | bytes 49152 | tf_op jit(solution)/shard_map/psum | solution.py:374
  (520 shorter events, 291.1 us)
Async XLA Ops:
  7.2 79.1 %all-gather.15.cloned.1.call-start = ((), (), s32[]{:S(2)}) async-start(), calls=%async_computation.16 | async-start | bytes 7864320 | tf_op jit(solution)/shard_map/all_gather | solution.py:170
  12.4 162.7 %copy-start.95 = (f32[1,1,512]{2,1,0:T(1,128)}, f32[1,1,512]{2,1,0:T(1,128)S(1)}, u32[]{:S(2)}) copy-start(f32[1,1,512]{2,1,0:T(1,128)S(1)} %get-tuple-element.137) | copy-start | bytes 6148
  15.6 92.5 %copy-start.115 = (pred[16,16]{1,0:T(8,128)(4,1)}, pred[16,16]{1,0:T(8,128)(4,1)S(1)}, u32[]{:S(2)}) copy-start(pred[16,16]{1,0:T(8,128)(4,1)S(1)} %iota_compare_fusion.1) | copy-start | bytes 772
  31.0 60.8 %copy-start.48 = (bf16[1,3,512,128]{3,2,1,0:T(8,128)(2,1)}, bf16[1,3,512,128]{3,2,1,0:T(8,128)(2,1)S(1)}, u32[]{:S(2)}) copy-start(bf16[1,3,512,128]{3,2,1,0:T(8,128)(2,1)S(1)} %all_gather.71) | copy-start | bytes 1179652
  109.0 15.5 copy-start.17
  127.2 12.0 copy-start.27
  132.9 10.5 copy-start.98
  139.2 30.0 %copy-start.112 = (f32[2,2,512]{2,1,0:T(2,128)S(1)}, f32[2,2,512]{2,1,0:T(2,128)}, u32[]{:S(2)}) copy-start(f32[2,2,512]{2,1,0:T(2,128)} %param.20) | copy-start | bytes 24580
  139.2 30.6 %all-to-all-start = ((bf16[4,1536,128]{2,1,0:T(8,128)(2,1)}), bf16[4,1536,128]{2,1,0:T(8,128)(2,1)S(1)}, u32[]{:S(2)}, u32[]{:S(2)}) async-start(bf16[4,1536,128]{2,1,0:T(8,128)(2,1)} %reshape.482), calls=%async_computation | async-start | bytes 3145728 | tf_op jit(solution)/shard_map/all_to_all | solution.py:245
  143.5 103.8 %all-gather.17.cloned.1.call-start = ((), (), s32[]{:S(2)}) async-start(), calls=%async_computation.17 | async-start | bytes 7864320 | tf_op jit(solution)/shard_map/all_gather | solution.py:170
  173.6 185.3 %copy-start = (f32[1536,512]{1,0:T(8,128)}, f32[1536,512]{1,0:T(8,128)S(1)}, u32[]{:S(2)}) copy-start(f32[1536,512]{1,0:T(8,128)S(1)} %get-tuple-element.114) | copy-start | bytes 9437188
  176.9 182.0 %reduce-scatter.21.cloned.1.call-start = ((), (), s32[]{:S(2)}) async-start(), calls=%async_computation.18 | async-start | bytes 7864320 | tf_op jit(solution)/shard_map/reduce_scatter | solution.py:192
  177.6 103.0 %copy-start.118 = (f32[1,512]{1,0:T(1,128)}, f32[1,512]{1,0:T(1,128)S(1)}, u32[]{:S(2)}) copy-start(f32[1,512]{1,0:T(1,128)S(1)} %get-tuple-element.145) | copy-start | bytes 6148
  247.2 36.1 %copy-start.58 = (bf16[1,512,512]{1,2,0:T(8,128)(2,1)S(1)}, bf16[1,512,512]{1,2,0:T(8,128)(2,1)}, u32[]{:S(2)}) copy-start(bf16[1,512,512]{1,2,0:T(8,128)(2,1)} %all_gather.76) | copy-start | bytes 1572868
  288.7 146.0 %all-gather.19.cloned.1.call-start = ((), (), s32[]{:S(2)}) async-start(), calls=%async_computation.19 | async-start | bytes 7864320 | tf_op jit(solution)/shard_map/all_gather | solution.py:170
  379.3 60.9 %copy-start.49 = (bf16[1,3,512,128]{3,2,1,0:T(8,128)(2,1)}, bf16[1,3,512,128]{3,2,1,0:T(8,128)(2,1)S(1)}, u32[]{:S(2)}) copy-start(bf16[1,3,512,128]{3,2,1,0:T(8,128)(2,1)S(1)} %all_gather.78) | copy-start | bytes 1179652
  457.3 15.6 copy-start.19
  475.7 12.0 copy-start.29
  481.4 11.1 copy-start.92
  487.7 32.7 %all-to-all-start.1 = ((bf16[4,1536,128]{2,1,0:T(8,128)(2,1)}), bf16[4,1536,128]{2,1,0:T(8,128)(2,1)}, u32[]{:S(2)}, u32[]{:S(2)}) async-start(bf16[4,1536,128]{2,1,0:T(8,128)(2,1)} %reshape.483), calls=%async_computation.2 | async-start | bytes 3145728 | tf_op jit(solution)/shard_map/all_to_all | solution.py:245
  492.5 106.3 %all-gather.21.cloned.1.call-start = ((), (), s32[]{:S(2)}) async-start(), calls=%async_computation.20 | async-start | bytes 7864320 | tf_op jit(solution)/shard_map/all_gather | solution.py:170
  527.9 18.0 %copy-start.69 = (bf16[1,512,64]{1,2,0:T(8,128)(2,1)S(1)}, bf16[1,512,64]{1,2,0:T(8,128)(2,1)}, u32[]{:S(2)}) copy-start(bf16[1,512,64]{1,2,0:T(8,128)(2,1)} %get-tuple-element.124) | copy-start | bytes 196612
  527.9 70.9 %copy-start.120 = (f32[1,512]{1,0:T(1,128)S(1)}, f32[1,512]{1,0:T(1,128)}, u32[]{:S(2)}) copy-start(f32[1,512]{1,0:T(1,128)} %get-tuple-element.144) | copy-start | bytes 6148
  527.9 142.8 %all-gather.23.cloned.1.call-start = ((), (), s32[]{:S(2)}) async-start(), calls=%async_computation.22 | async-start | bytes 7864320 | tf_op jit(solution)/shard_map/all_gather | solution.py:183
  530.7 232.4 %reduce-scatter.25.cloned.1.call-start = ((), (), s32[]{:S(2)}) async-start(), calls=%async_computation.23 | async-start | bytes 7864320 | tf_op jit(solution)/shard_map/reduce_scatter | solution.py:201
  692.9 143.4 %reduce-scatter.23.cloned.1.call-start = ((), (), s32[]{:S(2)}) async-start(), calls=%async_computation.21 | async-start | bytes 7864320 | tf_op jit(solution)/shard_map/reduce_scatter | solution.py:192
  701.2 61.9 %copy-start.6 = (f32[1536,512]{1,0:T(8,128)S(1)}, f32[1536,512]{1,0:T(8,128)}, u32[]{:S(2)}) copy-start(f32[1536,512]{1,0:T(8,128)} %copy-done.5) | copy-start | bytes 9437188
  701.3 213.7 %all-gather.25.cloned.1.call-start = ((), (), s32[]{:S(2)}) async-start(), calls=%async_computation.24 | async-start | bytes 7864320 | tf_op jit(solution)/shard_map/all_gather | solution.py:183
  766.4 69.9 %copy-start.107 = (f32[1,1,512]{2,1,0:T(1,128)S(1)}, f32[1,1,512]{2,1,0:T(1,128)}, u32[]{:S(2)}) copy-start(f32[1,1,512]{2,1,0:T(1,128)} %get-tuple-element.132) | copy-start | bytes 6148
  843.1 71.9 %copy-start.56 = (bf16[1,128,512]{1,2,0:T(8,128)(2,1)S(1)}, bf16[1,128,512]{1,2,0:T(8,128)(2,1)}, u32[]{:S(2)}) copy-start(bf16[1,128,512]{1,2,0:T(8,128)(2,1)} %copy-done.55) | copy-start | bytes 393220
  920.8 7.9 slice-start.2
  945.5 6.5 copy-start.24
  986.2 88.0 %all-to-all-start.2 = ((bf16[6144,3,128]{2,1,0:T(4,128)(2,1)}), bf16[6144,3,128]{2,1,0:T(4,128)(2,1)}, u32[]{:S(2)}, u32[]{:S(2)}) async-start(bf16[6144,3,128]{2,1,0:T(4,128)(2,1)} %copy.393), calls=%async_computation.5 | async-start | bytes 12582912 | tf_op jit(solution)/shard_map/all_to_all | solution.py:323
  992.0 69.1 %all-gather.31.cloned.1.call-start = ((), (), s32[]{:S(2)}) async-start(), calls=%async_computation.32 | async-start | bytes 1966080 | tf_op jit(solution)/shard_map/all_gather | solution.py:242
  992.6 170.6 %all-gather.27.cloned.1.call-start = ((), (), s32[]{:S(2)}) async-start(), calls=%async_computation.25 | async-start | bytes 7864320 | tf_op jit(solution)/shard_map/all_gather | solution.py:183
  1088.9 74.3 %copy-start.59 = (bf16[1,512,512]{1,2,0:T(8,128)(2,1)S(1)}, bf16[1,512,512]{1,2,0:T(8,128)(2,1)}, u32[]{:S(2)}) copy-start(bf16[1,512,512]{1,2,0:T(8,128)(2,1)} %all_gather.76) | copy-start | bytes 1572868
  1088.9 74.3 %copy-start.119 = (f32[1,512]{1,0:T(1,128)S(1)}, f32[1,512]{1,0:T(1,128)}, u32[]{:S(2)}) copy-start(f32[1,512]{1,0:T(1,128)} %copy-done.118) | copy-start | bytes 6148
  1090.2 164.6 %reduce-scatter.27.cloned.1.call-start = ((), (), s32[]{:S(2)}) async-start(), calls=%async_computation.26 | async-start | bytes 7864320 | tf_op jit(solution)/shard_map/reduce_scatter | solution.py:201
  1163.2 16.1 copy-start.57
  1184.6 103.1 %all-gather.33.cloned.1.call-start = ((), (), s32[]{:S(2)}) async-start(), calls=%async_computation.33 | async-start | bytes 1966080 | tf_op jit(solution)/shard_map/all_gather | solution.py:242
  1185.4 131.8 %reduce-scatter.43.cloned.1.call-start = ((), (), s32[]{:S(2)}) async-start(), calls=%async_computation.37 | async-start | bytes 589824
  1194.7 60.2 %copy-start.1 = (f32[1536,512]{1,0:T(8,128)S(1)}, f32[1536,512]{1,0:T(8,128)}, u32[]{:S(2)}) copy-start(f32[1536,512]{1,0:T(8,128)} %copy-done) | copy-start | bytes 9437188
  1194.7 60.2 %copy-start.67 = (f32[1536]{0:T(1024)S(1)}, f32[1536]{0:T(1024)}, u32[]{:S(2)}) copy-start(f32[1536]{0:T(1024)} %copy-done.66) | copy-start | bytes 18436
  1194.7 60.2 %copy-start.96 = (f32[1,1,512]{2,1,0:T(1,128)S(1)}, f32[1,1,512]{2,1,0:T(1,128)}, u32[]{:S(2)}) copy-start(f32[1,1,512]{2,1,0:T(1,128)} %copy-done.95) | copy-start | bytes 6148
  1198.4 59.1 %copy-start.89 = (f32[1536]{0:T(1024)S(1)}, f32[1536]{0:T(1024)}, u32[]{:S(2)}) copy-start(f32[1536]{0:T(1024)} %copy-done.88) | copy-start | bytes 18436
  1198.4 59.2 %copy-start.80 = (f32[1536]{0:T(1024)S(1)}, f32[1536]{0:T(1024)}, u32[]{:S(2)}) copy-start(f32[1536]{0:T(1024)} %copy-done.79) | copy-start | bytes 18436
  1200.8 190.2 %all-gather.29.cloned.1.call-start = ((), (), s32[]{:S(2)}) async-start(), calls=%async_computation.27 | async-start | bytes 7864320 | tf_op jit(solution)/shard_map/all_gather | solution.py:183
  1264.2 209.2 %reduce-scatter.39.cloned.1.call-start = ((), (), s32[]{:S(2)}) async-start(), calls=%async_computation.35 | async-start | bytes 147456
  1271.3 203.1 %reduce-scatter.41.cloned.1.call-start = ((), (), s32[]{:S(2)}) async-start(), calls=%async_computation.36 | async-start | bytes 589824
  1279.4 11.9 copy-start.28
  1281.3 11.0 copy-start.51
  1281.3 202.9 %reduce-scatter.35.cloned.1.call-start = ((), (), s32[]{:S(2)}) async-start(), calls=%async_computation.31 | async-start | bytes 589824 | tf_op jit(solution)/shard_map/reduce_scatter | solution.py:150
  1302.8 211.6 %reduce-scatter.33.cloned.1.call-start = ((), (), s32[]{:S(2)}) async-start(), calls=%async_computation.30 | async-start | bytes 589824 | tf_op jit(solution)/shard_map/reduce_scatter | solution.py:150
  1318.3 72.8 %copy-start.54 = (bf16[1,128,512]{1,2,0:T(8,128)(2,1)S(1)}, bf16[1,128,512]{1,2,0:T(8,128)(2,1)}, u32[]{:S(2)}) copy-start(bf16[1,128,512]{1,2,0:T(8,128)(2,1)} %copy-done.53) | copy-start | bytes 393220
  1396.8 8.1 slice-start
  1454.7 154.0 %all-to-all-start.3 = ((bf16[6144,3,128]{2,1,0:T(4,128)(2,1)}), bf16[6144,3,128]{2,1,0:T(4,128)(2,1)}, u32[]{:S(2)}, u32[]{:S(2)}) async-start(bf16[6144,3,128]{2,1,0:T(4,128)(2,1)} %copy.417), calls=%async_computation.7 | async-start | bytes 12582912 | tf_op jit(solution)/shard_map/all_to_all | solution.py:323
  1460.6 84.4 %reduce-scatter.37.cloned.1.call-start = ((), (), s32[]{:S(2)}) async-start(), calls=%async_computation.34 | async-start | bytes 147456
  1465.3 7.8 copy-start.122
  1465.3 7.9 copy-start.123
  1465.3 8.9 copy-start.117
  1465.3 110.7 %reduce-scatter.31.cloned.1.call-start = ((), (), s32[]{:S(2)}) async-start(), calls=%async_computation.29 | async-start | bytes 442368 | tf_op jit(solution)/shard_map/reduce_scatter | solution.py:144
  1473.3 133.8 %reduce-scatter.29.cloned.1.call-start = ((), (), s32[]{:S(2)}) async-start(), calls=%async_computation.28 | async-start | bytes 442368 | tf_op jit(solution)/shard_map/reduce_scatter | solution.py:144
  1476.4 39.6 %copy-start.103 = (f32[512]{0:T(512)S(1)}, f32[512]{0:T(512)}, u32[]{:S(2)}) copy-start(f32[512]{0:T(512)} %get-tuple-element.121) | copy-start | bytes 6148
  1476.4 39.6 %copy-start.104 = (f32[512]{0:T(512)S(1)}, f32[512]{0:T(512)}, u32[]{:S(2)}) copy-start(f32[512]{0:T(512)} %get-tuple-element.95) | copy-start | bytes 6148
  (95 other events, 291.1 us)
Sparse Core Ops, SparseCore 0:
  15.0 71.2 all-gather.14
  177.1 70.1 all-gather.16
  288.8 70.0 reduce-scatter.20
  364.3 70.3 all-gather.18
  528.0 70.7 all-gather.20
  600.5 70.1 all-gather.22
  693.0 70.0 reduce-scatter.24
  766.1 70.1 reduce-scatter.22
  844.6 70.3 all-gather.24
  994.3 66.7 all-gather.30
  1090.4 72.8 all-gather.26
  1184.8 70.0 reduce-scatter.26
  1256.7 30.9 all-gather.32
  1289.8 27.3 reduce-scatter.42
  1319.1 71.9 all-gather.28
  1393.8 26.6 reduce-scatter.38
  1422.6 28.9 reduce-scatter.40
  1453.8 29.1 reduce-scatter.34
  1485.3 29.0 reduce-scatter.32
  1516.5 28.3 reduce-scatter.36
  1547.2 28.7 reduce-scatter.30
  1578.4 28.7 reduce-scatter.28
where the time goes:
time: 1690 us; the launch traced here: 1670 us
  waiting for transfers between devices  890 us (53%)
  matrix products  278 us (16%)
  blocking collectives  200 us (12%)
  local copies, waits for them, and re-layouts  189 us (11%)
  other arithmetic  78.1 us (5%)
  starting transfers between devices  22.5 us (1%)
    all_gather x4, waiting for transfers between devices, spread_grads(): piece = lax.all_gather(rows, 'tensor', axis=0, tiled=True)  246 us
    all_gather x4, waiting for transfers between devices, spread_only(): return project(lax.all_gather(rows, 'tensor', axis=0, tiled=True))  185 us
    reduce_scatter x2, waiting for transfers between devices, rows_sum(): lax.psum_scatter(slice_term(source, weight, form).astype(jnp.bfloat16), '...  138 us
    reduce_scatter x2, waiting for transfers between devices, grads_sum(): lax.psum_scatter(slice_term(source, weight, form).astype(jnp.bfloat16), '...  115 us
    all_gather x2, waiting for transfers between devices, forward_layer(): lax.all_gather(w_qkv, 'tensor', axis=2, tiled=True)  74.7 us
    dot_general x2, matrix products, project_up(): return jnp.dot(piece, w_up, preferred_element_type=jnp.float32)  66.4 us
    reduce_scatter x2, waiting for transfers between devices, return_grads(): lax.psum_scatter(first.astype(jnp.bfloat16), 'dp', scatter_dimension=2, t...  60.6 us
    unnamed x296, local copies, waits for them, and re-layouts  59.3 us
  transfers between devices with their start and end apart: 26, of which 20 were waited for; matrix products, arithmetic and copies ran while one was open for 13% of the time, Pallas kernels for 0%

commit v1 on v0

--- a/solution.py
+++ b/solution.py
@@ -180,7 +180,15 @@
 
 
 def spread_grads(rows, project):
-    piece = lax.all_gather(rows, "tensor", axis=0, tiled=True)
+    ways, here = (lax.axis_size("tensor"), lax.axis_index("tensor"))
+    grown, reach = (rows, 1)
+    while reach < ways:
+        theirs = lax.ppermute(grown, "tensor", [(d, d ^ reach) for d in range(ways)])
+        mine_first = jnp.concatenate([grown, theirs], axis=0)
+        theirs_first = jnp.concatenate([theirs, grown], axis=0)
+        grown = jnp.where(here & reach == 0, mine_first, theirs_first)
+        reach = 2 * reach
+    piece = grown
     return (piece, project(piece))
 
 

time: 1690 us -> 1730 us (1.024)
  waiting for transfers between devices: 890 us -> 920 us
  other arithmetic: 78.1 us -> 96.1 us
    ppermute x0 -> x8, waiting for transfers between devices: none -> 364 us  [spread_grads(): lax.ppermute(grown, 'tensor', [(d, d ^ reach) for d in range(ways)])]
    all_gather x4 -> x0, waiting for transfers between devices: 246 us -> none  [spread_grads(): piece = lax.all_gather(rows, 'tensor', axis=0, tiled=True)]
    dot_general x2, matrix products: 27.5 us -> 63 us  [back_down(): jnp.einsum('td,fd->tf', piece, w_down, preferred_element_type=jnp.float32)]
    reduce_scatter x2, waiting for transfers between devices: 30.2 us -> 0.04 us  [return_grads(): lax.psum_scatter(third.astype(jnp.bfloat16), 'dp', scatter_dimension=1, t...]
    unnamed x26 -> x22, waiting for transfers between devices: 29.9 us -> 1.58 us
    dot_general x2, matrix products: 66.4 us -> 39.1 us  [project_up(): return jnp.dot(piece, w_up, preferred_element_type=jnp.float32)]
    all_gather x4, waiting for transfers between devices: 185 us -> 162 us  [spread_only(): return project(lax.all_gather(rows, 'tensor', axis=0, tiled=True))]
    unnamed x296 -> x320, local copies, waits for them, and re-layouts: 59.3 us -> 50.2 us
  transfers between devices with their start and end apart: 26 -> 30, of which waited for: 20 -> 20; matrix products, arithmetic and copies ran while one was open for 13% -> 12% of each run, Pallas kernels for 0% -> 0%
where the time goes in v1:
time: 1730 us; the launch traced here: 1720 us
  waiting for transfers between devices  920 us (53%)
  matrix products  284 us (16%)
  blocking collectives  200 us (12%)
  local copies, waits for them, and re-layouts  175 us (10%)
  other arithmetic  96.1 us (6%)
  starting transfers between devices  31.3 us (2%)
    ppermute x8, waiting for transfers between devices, spread_grads(): lax.ppermute(grown, 'tensor', [(d, d ^ reach) for d in range(ways)])  364 us
    all_gather x4, waiting for transfers between devices, spread_only(): return project(lax.all_gather(rows, 'tensor', axis=0, tiled=True))  162 us
    reduce_scatter x2, waiting for transfers between devices, rows_sum(): lax.psum_scatter(slice_term(source, weight, form).astype(jnp.bfloat16), '...  138 us
    reduce_scatter x2, waiting for transfers between devices, grads_sum(): lax.psum_scatter(slice_term(source, weight, form).astype(jnp.bfloat16), '...  123 us
    all_gather x2, waiting for transfers between devices, forward_layer(): lax.all_gather(w_qkv, 'tensor', axis=2, tiled=True)  66.6 us
    dot_general x2, matrix products, back_down(): jnp.einsum('td,fd->tf', piece, w_down, preferred_element_type=jnp.float32)  63 us
    reduce_scatter x2, waiting for transfers between devices, return_grads(): lax.psum_scatter(first.astype(jnp.bfloat16), 'dp', scatter_dimension=2, t...  54.7 us
    unnamed x320, local copies, waits for them, and re-layouts  50.2 us
  transfers between devices with their start and end apart: 30, of which 20 were waited for; matrix products, arithmetic and copies ran while one was open for 12% of the time, Pallas kernels for 0%

profile of v1, /device:TPU:12, one launch (start us, length us, event | category | flops | bytes accessed | tf_op | source)
XLA Modules:
  0.0 1723.4 jit_solution(11724684884710507020)
XLA Ops:
  16.3 14.7 all_gather.59
  31.0 55.3 %all-gather.11.cloned.1.call-done = bf16[6144,512]{1,0:T(8,128)(2,1)} async-done(((bf16[1536,512]{1,0:T(8,128)(2,1)}), bf16[6144,512]{1,0:T(8,128)(2,1)}) %all-gather.11.cloned.1.call-update) | async-done | bytes 6291472 | tf_op jit(solution)/shard_map/all_gather | solution.py:170
  86.3 5.5 fusion.18
  119.6 5.7 copy.448
  125.2 6.3 reshape.482
  136.4 14.0 all_gather.60
  151.0 10.7 all-gather
  171.6 15.7 all_gather.64
  187.3 15.9 all_gather.63
  203.2 36.8 %all-gather.13.cloned.1.call-done = bf16[6144,512]{1,0:T(8,128)(2,1)} async-done(((bf16[1536,512]{1,0:T(8,128)(2,1)}), bf16[6144,512]{1,0:T(8,128)(2,1)}) %all-gather.13.cloned.1.call-update) | async-done | bytes 6291472 | tf_op jit(solution)/shard_map/all_gather | solution.py:170
  239.9 33.3 %multiply_convert_fusion.1 = (bf16[6144,512]{1,0:T(8,128)(2,1)S(1)}, f32[6144,512]{1,0:T(8,128)}, f32[6144,512]{1,0:T(8,128)}) fusion(f32[512]{0:T(512)S(1)} %bitcast.502, bf16[6144,512]{1,0:T(8,128)(2,1)} %all-gather.13.cloned.1.call-done, bf16[1,512,512]{2,1,0:T(8,128)(2,1)} %all_gather.63), kind=kOutput, calls=%fused_computation.28 | convolution fusion | flops 3428843520 | bytes 38275072 | tf_op jit(solution)/shard_map/dot_general | solution.py:241
  276.0 5.4 convolution_convert_fusion.3
  281.5 70.2 %reduce-scatter.21.cloned.1.call-done = bf16[1536,512]{1,0:T(8,128)(2,1)} async-done(((bf16[6144,512]{1,0:T(8,128)(2,1)}), bf16[1536,512]{1,0:T(8,128)(2,1)}) %reduce-scatter.21.cloned.1.call-update) | async-done | bytes 1572880 | tf_op jit(solution)/shard_map/reduce_scatter | solution.py:200
  357.1 14.7 all_gather.66
  371.9 55.6 %all-gather.15.cloned.1.call-done = bf16[6144,512]{1,0:T(8,128)(2,1)} async-done(((bf16[1536,512]{1,0:T(8,128)(2,1)}), bf16[6144,512]{1,0:T(8,128)(2,1)}) %all-gather.15.cloned.1.call-update) | async-done | bytes 6291472 | tf_op jit(solution)/shard_map/all_gather | solution.py:170
  427.4 5.5 fusion.14
  460.6 5.7 copy.449
  466.4 6.3 reshape.483
  477.6 14.0 all_gather.67
  492.2 11.3 all-gather.1
  517.4 54.7 %collective-permute-done = bf16[1536,512]{1,0:T(8,128)(2,1)} collective-permute-done((bf16[1536,512]{1,0:T(8,128)(2,1)}, bf16[1536,512]{1,0:T(8,128)(2,1)}, u32[]{:S(2)}, u32[]{:S(2)}) %collective-permute-start) | collective-permute-done | bytes 1572896 | tf_op jit(solution)/shard_map/ppermute | solution.py:186
  577.9 15.7 all_gather.71
  593.6 15.9 all_gather.70
  609.5 14.5 all-gather.17.cloned.1.call-done
  624.0 5.8 fusion.211
  629.8 37.2 %collective-permute-done.1 = bf16[3072,512]{1,0:T(8,128)(2,1)} collective-permute-done((bf16[3072,512]{1,0:T(8,128)(2,1)S(1)}, bf16[3072,512]{1,0:T(8,128)(2,1)}, u32[]{:S(2)}, u32[]{:S(2)}) %collective-permute-start.1) | collective-permute-done | bytes 3145760 | tf_op jit(solution)/shard_map/ppermute | solution.py:186
  667.0 41.9 %convert_reduce_fusion.4 = (f32[512]{0:T(512)}, bf16[6144,512]{1,0:T(8,128)(2,1)S(1)}, f32[6144,512]{1,0:T(8,128)}) fusion(f32[6144,512]{1,0:T(8,128)S(1)} %fusion.211, f32[512]{0:T(512)S(1)} %bitcast.481, bf16[1,512,512]{1,2,0:T(8,128)(2,1)S(1)} %copy-done.67, bf16[3072,512]{1,0:T(8,128)(2,1)} %collective-permute-done.1, ...), kind=kOutput, calls=%fused_computation.10 | convolution fusion | flops 3485466112 | bytes 38277120 | tf_op jit(solution)/shard_map/td,fd->tf/dot_general | solution.py:301
  711.5 5.3 convolution_convert_fusion.1
  717.1 10.2 multiply_convert_fusion
  730.0 5.4 convolution_convert_fusion.2
  735.5 52.6 %reduce-scatter.25.cloned.1.call-done = bf16[1536,512]{1,0:T(8,128)(2,1)} async-done(((bf16[6144,512]{1,0:T(8,128)(2,1)}), bf16[1536,512]{1,0:T(8,128)(2,1)}) %reduce-scatter.25.cloned.1.call-update) | async-done | bytes 1572880 | tf_op jit(solution)/shard_map/reduce_scatter | solution.py:209
  793.8 67.4 %reduce-scatter.23.cloned.1.call-done = bf16[1536,512]{1,0:T(8,128)(2,1)} async-done(((bf16[6144,512]{1,0:T(8,128)(2,1)}), bf16[1536,512]{1,0:T(8,128)(2,1)}) %reduce-scatter.23.cloned.1.call-update) | async-done | bytes 1572880 | tf_op jit(solution)/shard_map/reduce_scatter | solution.py:200
  867.3 35.4 %collective-permute-done.2 = bf16[1536,512]{1,0:T(8,128)(2,1)S(1)} collective-permute-done((bf16[1536,512]{1,0:T(8,128)(2,1)S(1)}, bf16[1536,512]{1,0:T(8,128)(2,1)S(1)}, u32[]{:S(2)}, u32[]{:S(2)}) %collective-permute-start.2) | collective-permute-done | bytes 1572896 | tf_op jit(solution)/shard_map/ppermute | solution.py:186
  904.5 68.2 %collective-permute-done.3 = bf16[3072,512]{1,0:T(8,128)(2,1)S(1)} collective-permute-done((bf16[3072,512]{1,0:T(8,128)(2,1)S(1)}, bf16[3072,512]{1,0:T(8,128)(2,1)S(1)}, u32[]{:S(2)}, u32[]{:S(2)}) %collective-permute-start.3) | collective-permute-done | bytes 3145760 | tf_op jit(solution)/shard_map/ppermute | solution.py:186
  974.4 6.9 convolution_convert_fusion.5
  1006.4 6.7 multiply_convert_fusion.3
  1033.1 10.1 copy.393
  1043.3 5.9 all-to-all-start.2
  1049.9 66.6 %all-gather.19.cloned.1.call-done = bf16[1,3,512,512]{3,2,1,0:T(8,128)(2,1)} async-done(((bf16[1,3,512,128]{3,2,1,0:T(8,128)(2,1)}), bf16[1,3,512,512]{3,2,1,0:T(8,128)(2,1)}) %all-gather.19.cloned.1.call-update) | async-done | bytes 1572880 | tf_op jit(solution)/shard_map/all_gather | solution.py:250
  1118.9 10.7 all-to-all-done.2
  1133.2 5.1 convert_reduce_fusion.2
  1146.5 34.6 %collective-permute-done.4 = bf16[1536,512]{1,0:T(8,128)(2,1)S(1)} collective-permute-done((bf16[1536,512]{1,0:T(8,128)(2,1)S(1)}, bf16[1536,512]{1,0:T(8,128)(2,1)S(1)}, u32[]{:S(2)}, u32[]{:S(2)}) %collective-permute-start.4) | collective-permute-done | bytes 1572896 | tf_op jit(solution)/shard_map/ppermute | solution.py:186
  1182.2 69.5 %collective-permute-done.5 = bf16[3072,512]{1,0:T(8,128)(2,1)S(1)} collective-permute-done((bf16[3072,512]{1,0:T(8,128)(2,1)S(1)}, bf16[3072,512]{1,0:T(8,128)(2,1)S(1)}, u32[]{:S(2)}, u32[]{:S(2)}) %collective-permute-start.5) | collective-permute-done | bytes 3145760 | tf_op jit(solution)/shard_map/ppermute | solution.py:186
  1251.7 21.1 %convert_reduce_fusion.5 = (f32[512]{0:T(512)S(1)}, bf16[6144,512]{1,0:T(8,128)(2,1)}) fusion(f32[6144,512]{1,0:T(8,128)} %get-tuple-element.115, f32[6144,512]{1,0:T(8,128)} %get-tuple-element.153, f32[512]{0:T(512)S(1)} %bitcast.503, bf16[1,512,512]{1,2,0:T(8,128)(2,1)S(1)} %copy-done.66, bf16[3072,512]{1,0:T(8,128)(2,1)S(1)} %collective-permute-done.5, ...), kind=kOutput, calls=%fused_computation.11 | convolution fusion | flops 3303013888 | bytes 38277120 | tf_op jit(solution)/shard_map/td,fd->tf/dot_general | solution.py:301
  1272.9 8.5 convolution_convert_fusion
  1282.1 70.4 %reduce-scatter.27.cloned.1.call-done = bf16[1536,512]{1,0:T(8,128)(2,1)} async-done(((bf16[6144,512]{1,0:T(8,128)(2,1)}), bf16[1536,512]{1,0:T(8,128)(2,1)}) %reduce-scatter.27.cloned.1.call-update) | async-done | bytes 1572880 | tf_op jit(solution)/shard_map/reduce_scatter | solution.py:209
  1362.5 7.8 fusion.149
  1373.9 5.9 fusion.161
  1380.7 30.2 %collective-permute-done.6 = bf16[1536,512]{1,0:T(8,128)(2,1)} collective-permute-done((bf16[1536,512]{1,0:T(8,128)(2,1)}, bf16[1536,512]{1,0:T(8,128)(2,1)}, u32[]{:S(2)}, u32[]{:S(2)}) %collective-permute-start.6) | collective-permute-done | bytes 1572896 | tf_op jit(solution)/shard_map/ppermute | solution.py:186
  1416.2 7.1 fusion.148
  1433.1 8.8 fusion.147
  1443.1 8.9 fusion.146
  1452.0 33.8 %collective-permute-done.7 = bf16[3072,512]{1,0:T(8,128)(2,1)} collective-permute-done((bf16[3072,512]{1,0:T(8,128)(2,1)}, bf16[3072,512]{1,0:T(8,128)(2,1)}, u32[]{:S(2)}, u32[]{:S(2)}) %collective-permute-start.7) | collective-permute-done | bytes 3145760 | tf_op jit(solution)/shard_map/ppermute | solution.py:186
  1485.9 7.5 convolution_convert_fusion.4
  1517.5 6.6 multiply_convert_fusion.2
  1543.5 10.2 copy.417
  1553.7 5.8 all-to-all-start.3
  1559.6 6.0 fusion.160
  1566.5 7.7 fusion.150
  1577.4 7.7 fusion.155
  1587.1 12.7 all-reduce.1
  1601.4 23.7 %reduce-scatter.31.cloned.1.call-done = bf16[1,3,64,128]{3,2,1,0:T(8,128)(2,1)} async-done(((bf16[1,3,512,128]{3,2,1,0:T(8,128)(2,1)}), bf16[1,3,64,128]{3,2,1,0:T(8,128)(2,1)}) %reduce-scatter.31.cloned.1.call-update) | async-done | bytes 49168 | tf_op jit(solution)/shard_map/reduce_scatter | solution.py:144
  1625.1 31.0 %reduce-scatter.29.cloned.1.call-done = bf16[1,3,64,128]{3,2,1,0:T(8,128)(2,1)} async-done(((bf16[1,3,512,128]{3,2,1,0:T(8,128)(2,1)}), bf16[1,3,64,128]{3,2,1,0:T(8,128)(2,1)}) %reduce-scatter.29.cloned.1.call-update) | async-done | bytes 49168 | tf_op jit(solution)/shard_map/reduce_scatter | solution.py:144
  1671.7 44.4 %all-reduce = (f32[2,2,512]{2,1,0:T(2,128)}, f32[2,2,512]{2,1,0:T(2,128)}, f32[2,2,512]{2,1,0:T(2,128)}) all-reduce(f32[2,2,512]{2,1,0:T(2,128)S(1)} %pad_maximum_fusion, f32[2,2,512]{2,1,0:T(2,128)S(1)} %pad_maximum_fusion.1, f32[2,2,512]{2,1,0:T(2,128)S(1)} %pad_maximum_fusion.2), channel_id=1, replica_groups=mesh['dp'=8,'tensor'=4] {'dp','tensor'}, use_global_device_ids=true, to_apply=%region_52.53 | all-reduce | flops 6144 | bytes 49152 | tf_op jit(solution)/shard_map/psum | solution.py:382
  (553 shorter events, 291.7 us)
Async XLA Ops:
  7.2 79.1 %all-gather.11.cloned.1.call-start = ((), (), s32[]{:S(2)}) async-start(), calls=%async_computation.16 | async-start | bytes 7864320 | tf_op jit(solution)/shard_map/all_gather | solution.py:170
  12.5 155.4 %copy-start.104 = (f32[1,1,512]{2,1,0:T(1,128)}, f32[1,1,512]{2,1,0:T(1,128)S(1)}, u32[]{:S(2)}) copy-start(f32[1,1,512]{2,1,0:T(1,128)S(1)} %get-tuple-element.140) | copy-start | bytes 6148
  15.7 95.9 %copy-start.126 = (pred[16,16]{1,0:T(8,128)(4,1)}, pred[16,16]{1,0:T(8,128)(4,1)S(1)}, u32[]{:S(2)}) copy-start(pred[16,16]{1,0:T(8,128)(4,1)S(1)} %iota_compare_fusion.1) | copy-start | bytes 772
  31.0 60.8 %copy-start.48 = (bf16[1,3,512,128]{3,2,1,0:T(8,128)(2,1)}, bf16[1,3,512,128]{3,2,1,0:T(8,128)(2,1)S(1)}, u32[]{:S(2)}) copy-start(bf16[1,3,512,128]{3,2,1,0:T(8,128)(2,1)S(1)} %all_gather.59) | copy-start | bytes 1179652
  131.5 30.4 %copy-start.123 = (f32[2,2,512]{2,1,0:T(2,128)S(1)}, f32[2,2,512]{2,1,0:T(2,128)}, u32[]{:S(2)}) copy-start(f32[2,2,512]{2,1,0:T(2,128)} %param.20) | copy-start | bytes 24580
  131.5 31.0 %all-to-all-start = ((bf16[4,1536,128]{2,1,0:T(8,128)(2,1)}), bf16[4,1536,128]{2,1,0:T(8,128)(2,1)S(1)}, u32[]{:S(2)}, u32[]{:S(2)}) async-start(bf16[4,1536,128]{2,1,0:T(8,128)(2,1)} %reshape.482), calls=%async_computation | async-start | bytes 3145728 | tf_op jit(solution)/shard_map/all_to_all | solution.py:253
  135.7 104.2 %all-gather.13.cloned.1.call-start = ((), (), s32[]{:S(2)}) async-start(), calls=%async_computation.17 | async-start | bytes 7864320 | tf_op jit(solution)/shard_map/all_gather | solution.py:170
  166.3 185.4 %copy-start = (f32[1536,512]{1,0:T(8,128)}, f32[1536,512]{1,0:T(8,128)S(1)}, u32[]{:S(2)}) copy-start(f32[1536,512]{1,0:T(8,128)S(1)} %get-tuple-element.117) | copy-start | bytes 9437188
  169.7 182.0 %reduce-scatter.21.cloned.1.call-start = ((), (), s32[]{:S(2)}) async-start(), calls=%async_computation.18 | async-start | bytes 7864320 | tf_op jit(solution)/shard_map/reduce_scatter | solution.py:200
  170.3 102.9 %copy-start.129 = (f32[1,512]{1,0:T(1,128)}, f32[1,512]{1,0:T(1,128)S(1)}, u32[]{:S(2)}) copy-start(f32[1,512]{1,0:T(1,128)S(1)} %get-tuple-element.148) | copy-start | bytes 6148
  239.9 36.1 %copy-start.65 = (bf16[1,512,512]{1,2,0:T(8,128)(2,1)S(1)}, bf16[1,512,512]{1,2,0:T(8,128)(2,1)}, u32[]{:S(2)}) copy-start(bf16[1,512,512]{1,2,0:T(8,128)(2,1)} %all_gather.64) | copy-start | bytes 1572868
  281.4 146.0 %all-gather.15.cloned.1.call-start = ((), (), s32[]{:S(2)}) async-start(), calls=%async_computation.19 | async-start | bytes 7864320 | tf_op jit(solution)/shard_map/all_gather | solution.py:170
  371.9 61.1 %copy-start.49 = (bf16[1,3,512,128]{3,2,1,0:T(8,128)(2,1)}, bf16[1,3,512,128]{3,2,1,0:T(8,128)(2,1)S(1)}, u32[]{:S(2)}) copy-start(bf16[1,3,512,128]{3,2,1,0:T(8,128)(2,1)S(1)} %all_gather.66) | copy-start | bytes 1179652
  472.7 33.1 %all-to-all-start.1 = ((bf16[4,1536,128]{2,1,0:T(8,128)(2,1)}), bf16[4,1536,128]{2,1,0:T(8,128)(2,1)}, u32[]{:S(2)}, u32[]{:S(2)}) async-start(bf16[4,1536,128]{2,1,0:T(8,128)(2,1)} %reshape.483), calls=%async_computation.2 | async-start | bytes 3145728 | tf_op jit(solution)/shard_map/all_to_all | solution.py:253
  477.5 146.4 %all-gather.17.cloned.1.call-start = ((), (), s32[]{:S(2)}) async-start(), calls=%async_computation.20 | async-start | bytes 7864320 | tf_op jit(solution)/shard_map/all_gather | solution.py:170
  513.3 274.7 %reduce-scatter.25.cloned.1.call-start = ((), (), s32[]{:S(2)}) async-start(), calls=%async_computation.22 | async-start | bytes 7864320 | tf_op jit(solution)/shard_map/reduce_scatter | solution.py:209
  516.1 55.9 %collective-permute-start = (bf16[1536,512]{1,0:T(8,128)(2,1)}, bf16[1536,512]{1,0:T(8,128)(2,1)}, u32[]{:S(2)}, u32[]{:S(2)}) collective-permute-start(bf16[1536,512]{1,0:T(8,128)(2,1)} %get-tuple-element.125), channel_id=1, source_target_pairs={{0,1},{1,0},{2,3},{3,2},{4,5},{5,4},{6,7},{7,6},{8,9},{9,8},{10,11... | collective-permute-start | bytes 4718600 | tf_op jit(solution)/shard_map/ppermute | solution.py:186
  517.4 60.5 %copy-start.78 = (bf16[1,512,64]{1,2,0:T(8,128)(2,1)S(1)}, bf16[1,512,64]{1,2,0:T(8,128)(2,1)}, u32[]{:S(2)}) copy-start(bf16[1,512,64]{1,2,0:T(8,128)(2,1)} %get-tuple-element.129) | copy-start | bytes 196612
  517.4 76.2 %copy-start.77 = (bf16[1,64,512]{2,1,0:T(8,128)(2,1)S(1)}, bf16[1,64,512]{2,1,0:T(8,128)(2,1)}, u32[]{:S(2)}) copy-start(bf16[1,64,512]{2,1,0:T(8,128)(2,1)} %get-tuple-element.127) | copy-start | bytes 196612
  575.3 91.7 %copy-start.50 = (bf16[3072,512]{1,0:T(8,128)(2,1)}, bf16[3072,512]{1,0:T(8,128)(2,1)S(1)}, u32[]{:S(2)}) copy-start(bf16[3072,512]{1,0:T(8,128)(2,1)S(1)} %maximum_select_fusion.4) | copy-start | bytes 9437188
  575.3 91.7 %collective-permute-start.1 = (bf16[3072,512]{1,0:T(8,128)(2,1)S(1)}, bf16[3072,512]{1,0:T(8,128)(2,1)}, u32[]{:S(2)}, u32[]{:S(2)}) collective-permute-start(bf16[3072,512]{1,0:T(8,128)(2,1)S(1)} %maximum_select_fusion.4), channel_id=1, source_target_pairs={{0,2},{1,3},{2,0},{3,1},{4,6},{5,7},{6,4},{7,5},{8,10},{9,11},{10,... | collective-permute-start | bytes 9437192 | tf_op jit(solution)/shard_map/ppermute | solution.py:186
  609.5 57.6 %copy-start.110 = (f32[1,512]{1,0:T(1,128)S(1)}, f32[1,512]{1,0:T(1,128)}, u32[]{:S(2)}) copy-start(f32[1,512]{1,0:T(1,128)} %get-tuple-element.147) | copy-start | bytes 6148
  624.0 43.0 %copy-start.67 = (bf16[1,512,512]{1,2,0:T(8,128)(2,1)S(1)}, bf16[1,512,512]{1,2,0:T(8,128)(2,1)}, u32[]{:S(2)}) copy-start(bf16[1,512,512]{1,2,0:T(8,128)(2,1)} %all_gather.71) | copy-start | bytes 1572868
  629.8 79.2 %copy-start.11 = (f32[6144,512]{1,0:T(8,128)}, f32[6144,512]{1,0:T(8,128)S(1)}, u32[]{:S(2)}) copy-start(f32[6144,512]{1,0:T(8,128)S(1)} %fusion.211) | copy-start | bytes 37748740
  667.0 44.5 %copy-start.55 = (bf16[1,512,512]{2,1,0:T(8,128)(2,1)S(1)}, bf16[1,512,512]{2,1,0:T(8,128)(2,1)}, u32[]{:S(2)}) copy-start(bf16[1,512,512]{2,1,0:T(8,128)(2,1)} %all_gather.70) | copy-start | bytes 1572868
  716.9 144.3 %reduce-scatter.23.cloned.1.call-start = ((), (), s32[]{:S(2)}) async-start(), calls=%async_computation.21 | async-start | bytes 7864320 | tf_op jit(solution)/shard_map/reduce_scatter | solution.py:200
  735.4 52.6 %copy-start.6 = (f32[1536,512]{1,0:T(8,128)S(1)}, f32[1536,512]{1,0:T(8,128)}, u32[]{:S(2)}) copy-start(f32[1536,512]{1,0:T(8,128)} %copy-done.5) | copy-start | bytes 9437188
  791.2 70.0 %copy-start.118 = (f32[1,1,512]{2,1,0:T(1,128)S(1)}, f32[1,1,512]{2,1,0:T(1,128)}, u32[]{:S(2)}) copy-start(f32[1,1,512]{2,1,0:T(1,128)} %get-tuple-element.135) | copy-start | bytes 6148
  866.3 37.4 %copy-start.14 = (f32[1536,512]{1,0:T(8,128)}, f32[1536,512]{1,0:T(8,128)S(1)}, u32[]{:S(2)}) copy-start(f32[1536,512]{1,0:T(8,128)S(1)} %get-tuple-element.101) | copy-start | bytes 9437188
  866.5 38.0 %copy-start.59 = (f32[3,16,2,128]{3,1,2,0:T(8,128)S(1)}, f32[3,16,2,128]{3,1,2,0:T(8,128)}, u32[]{:S(2)}) copy-start(f32[3,16,2,128]{3,1,2,0:T(8,128)} %get-tuple-element.106) | copy-start | bytes 147460
  866.5 107.9 %copy-start.63 = (bf16[1,128,512]{1,2,0:T(8,128)(2,1)S(1)}, bf16[1,128,512]{1,2,0:T(8,128)(2,1)}, u32[]{:S(2)}) copy-start(bf16[1,128,512]{1,2,0:T(8,128)(2,1)} %copy-done.62) | copy-start | bytes 393220
  866.5 36.2 %collective-permute-start.2 = (bf16[1536,512]{1,0:T(8,128)(2,1)S(1)}, bf16[1536,512]{1,0:T(8,128)(2,1)S(1)}, u32[]{:S(2)}, u32[]{:S(2)}) collective-permute-start(bf16[1536,512]{1,0:T(8,128)(2,1)S(1)} %convert_element_type.442), channel_id=1, source_target_pairs={{0,1},{1,0},{2,3},{3,2},{4,5},{5,4},{6,7},{7,6},{8,9},{9,8},{10,11... | collective-permute-start | bytes 4718600 | tf_op jit(solution)/shard_map/ppermute | solution.py:186
  903.7 69.1 %copy-start.52 = (bf16[3072,512]{1,0:T(8,128)(2,1)}, bf16[3072,512]{1,0:T(8,128)(2,1)S(1)}, u32[]{:S(2)}) copy-start(bf16[3072,512]{1,0:T(8,128)(2,1)S(1)} %maximum_select_fusion.5) | copy-start | bytes 9437188
  903.7 69.0 %collective-permute-start.3 = (bf16[3072,512]{1,0:T(8,128)(2,1)S(1)}, bf16[3072,512]{1,0:T(8,128)(2,1)S(1)}, u32[]{:S(2)}, u32[]{:S(2)}) collective-permute-start(bf16[3072,512]{1,0:T(8,128)(2,1)S(1)} %maximum_select_fusion.5), channel_id=1, source_target_pairs={{0,2},{1,3},{2,0},{3,1},{4,6},{5,7},{6,4},{7,5},{8,10},{9,11},{10,... | collective-permute-start | bytes 9437192 | tf_op jit(solution)/shard_map/ppermute | solution.py:186
  1043.3 86.4 %all-to-all-start.2 = ((bf16[6144,3,128]{2,1,0:T(4,128)(2,1)}), bf16[6144,3,128]{2,1,0:T(4,128)(2,1)}, u32[]{:S(2)}, u32[]{:S(2)}) async-start(bf16[6144,3,128]{2,1,0:T(4,128)(2,1)} %copy.393), calls=%async_computation.5 | async-start | bytes 12582912 | tf_op jit(solution)/shard_map/all_to_all | solution.py:331
  1049.1 67.4 %all-gather.19.cloned.1.call-start = ((), (), s32[]{:S(2)}) async-start(), calls=%async_computation.28 | async-start | bytes 1966080 | tf_op jit(solution)/shard_map/all_gather | solution.py:250
  1049.9 302.6 %reduce-scatter.27.cloned.1.call-start = ((), (), s32[]{:S(2)}) async-start(), calls=%async_computation.23 | async-start | bytes 7864320 | tf_op jit(solution)/shard_map/reduce_scatter | solution.py:209
  1143.2 38.9 %copy-start.16 = (f32[1536,512]{1,0:T(8,128)}, f32[1536,512]{1,0:T(8,128)S(1)}, u32[]{:S(2)}) copy-start(f32[1536,512]{1,0:T(8,128)S(1)} %get-tuple-element.99) | copy-start | bytes 9437188
  1143.4 108.3 %copy-start.66 = (bf16[1,512,512]{1,2,0:T(8,128)(2,1)S(1)}, bf16[1,512,512]{1,2,0:T(8,128)(2,1)}, u32[]{:S(2)}) copy-start(bf16[1,512,512]{1,2,0:T(8,128)(2,1)} %all_gather.64) | copy-start | bytes 1572868
  1143.4 108.3 %copy-start.130 = (f32[1,512]{1,0:T(1,128)S(1)}, f32[1,512]{1,0:T(1,128)}, u32[]{:S(2)}) copy-start(f32[1,512]{1,0:T(1,128)} %copy-done.129) | copy-start | bytes 6148
  1143.4 37.7 %collective-permute-start.4 = (bf16[1536,512]{1,0:T(8,128)(2,1)S(1)}, bf16[1536,512]{1,0:T(8,128)(2,1)S(1)}, u32[]{:S(2)}, u32[]{:S(2)}) collective-permute-start(bf16[1536,512]{1,0:T(8,128)(2,1)S(1)} %convert_element_type.456), channel_id=1, source_target_pairs={{0,1},{1,0},{2,3},{3,2},{4,5},{5,4},{6,7},{7,6},{8,9},{9,8},{10,11... | collective-permute-start | bytes 4718600 | tf_op jit(solution)/shard_map/ppermute | solution.py:186
  1182.1 90.8 %copy-start.53 = (bf16[3072,512]{1,0:T(8,128)(2,1)}, bf16[3072,512]{1,0:T(8,128)(2,1)S(1)}, u32[]{:S(2)}) copy-start(bf16[3072,512]{1,0:T(8,128)(2,1)S(1)} %maximum_select_fusion.6) | copy-start | bytes 9437188
  1182.1 69.6 %collective-permute-start.5 = (bf16[3072,512]{1,0:T(8,128)(2,1)S(1)}, bf16[3072,512]{1,0:T(8,128)(2,1)S(1)}, u32[]{:S(2)}, u32[]{:S(2)}) collective-permute-start(bf16[3072,512]{1,0:T(8,128)(2,1)S(1)} %maximum_select_fusion.6), channel_id=1, source_target_pairs={{0,2},{1,3},{2,0},{3,1},{4,6},{5,7},{6,4},{7,5},{8,10},{9,11},{10,... | collective-permute-start | bytes 9437192 | tf_op jit(solution)/shard_map/ppermute | solution.py:186
  1251.7 21.2 %copy-start.137 = (bf16[3072,512]{1,0:T(8,128)(2,1)}, bf16[3072,512]{1,0:T(8,128)(2,1)S(1)}, u32[]{:S(2)}) copy-start(bf16[3072,512]{1,0:T(8,128)(2,1)S(1)} %collective-permute-done.5) | copy-start | bytes 9437188
  1281.4 71.1 %copy-start.1 = (f32[1536,512]{1,0:T(8,128)S(1)}, f32[1536,512]{1,0:T(8,128)}, u32[]{:S(2)}) copy-start(f32[1536,512]{1,0:T(8,128)} %copy-done) | copy-start | bytes 9437188
  1281.4 71.1 %copy-start.76 = (f32[1536]{0:T(1024)S(1)}, f32[1536]{0:T(1024)}, u32[]{:S(2)}) copy-start(f32[1536]{0:T(1024)} %copy-done.75) | copy-start | bytes 18436
  1281.4 71.1 %copy-start.105 = (f32[1,1,512]{2,1,0:T(1,128)S(1)}, f32[1,1,512]{2,1,0:T(1,128)}, u32[]{:S(2)}) copy-start(f32[1,1,512]{2,1,0:T(1,128)} %copy-done.104) | copy-start | bytes 6148
  1281.4 73.8 %copy-start.98 = (f32[1536]{0:T(1024)S(1)}, f32[1536]{0:T(1024)}, u32[]{:S(2)}) copy-start(f32[1536]{0:T(1024)} %copy-done.97) | copy-start | bytes 18436
  1281.4 73.8 %copy-start.89 = (f32[1536]{0:T(1024)S(1)}, f32[1536]{0:T(1024)}, u32[]{:S(2)}) copy-start(f32[1536]{0:T(1024)} %copy-done.88) | copy-start | bytes 18436
  1281.4 145.4 %all-gather.21.cloned.1.call-start = ((), (), s32[]{:S(2)}) async-start(), calls=%async_computation.29 | async-start | bytes 1966080 | tf_op jit(solution)/shard_map/all_gather | solution.py:250
  1282.0 159.9 %reduce-scatter.43.cloned.1.call-start = ((), (), s32[]{:S(2)}) async-start(), calls=%async_computation.33 | async-start | bytes 589824
  1361.8 49.1 %collective-permute-start.6 = (bf16[1536,512]{1,0:T(8,128)(2,1)}, bf16[1536,512]{1,0:T(8,128)(2,1)}, u32[]{:S(2)}, u32[]{:S(2)}) collective-permute-start(bf16[1536,512]{1,0:T(8,128)(2,1)} %convert_element_type.460), channel_id=1, source_target_pairs={{0,1},{1,0},{2,3},{3,2},{4,5},{5,4},{6,7},{7,6},{8,9},{9,8},{10,11... | collective-permute-start | bytes 4718600 | tf_op jit(solution)/shard_map/ppermute | solution.py:186
  1372.1 202.3 %reduce-scatter.39.cloned.1.call-start = ((), (), s32[]{:S(2)}) async-start(), calls=%async_computation.31 | async-start | bytes 147456
  1380.7 35.6 %copy-start.54 = (bf16[3072,512]{1,0:T(8,128)(2,1)S(1)}, bf16[3072,512]{1,0:T(8,128)(2,1)}, u32[]{:S(2)}) copy-start(bf16[3072,512]{1,0:T(8,128)(2,1)} %copy-done.53) | copy-start | bytes 9437188
  1380.7 194.7 %reduce-scatter.41.cloned.1.call-start = ((), (), s32[]{:S(2)}) async-start(), calls=%async_computation.32 | async-start | bytes 589824
  1380.7 35.5 %copy-start.138 = (bf16[3072,512]{1,0:T(8,128)(2,1)S(1)}, bf16[3072,512]{1,0:T(8,128)(2,1)}, u32[]{:S(2)}) copy-start(bf16[3072,512]{1,0:T(8,128)(2,1)} %copy-done.137) | copy-start | bytes 9437188
  1415.7 70.2 %collective-permute-start.7 = (bf16[3072,512]{1,0:T(8,128)(2,1)}, bf16[3072,512]{1,0:T(8,128)(2,1)}, u32[]{:S(2)}, u32[]{:S(2)}) collective-permute-start(bf16[3072,512]{1,0:T(8,128)(2,1)} %maximum_select_fusion.7), channel_id=1, source_target_pairs={{0,2},{1,3},{2,0},{3,1},{4,6},{5,7},{6,4},{7,5},{8,10},{9,11},{10,... | collective-permute-start | bytes 9437192 | tf_op jit(solution)/shard_map/ppermute | solution.py:186
  1426.8 158.4 %reduce-scatter.35.cloned.1.call-start = ((), (), s32[]{:S(2)}) async-start(), calls=%async_computation.27 | async-start | bytes 589824 | tf_op jit(solution)/shard_map/reduce_scatter | solution.py:150
  1441.9 143.3 %reduce-scatter.33.cloned.1.call-start = ((), (), s32[]{:S(2)}) async-start(), calls=%async_computation.26 | async-start | bytes 589824 | tf_op jit(solution)/shard_map/reduce_scatter | solution.py:150
  1443.1 42.8 %copy-start.61 = (bf16[1,128,512]{1,2,0:T(8,128)(2,1)S(1)}, bf16[1,128,512]{1,2,0:T(8,128)(2,1)}, u32[]{:S(2)}) copy-start(bf16[1,128,512]{1,2,0:T(8,128)(2,1)} %copy-done.60) | copy-start | bytes 393220
  1553.7 103.8 %all-to-all-start.3 = ((bf16[6144,3,128]{2,1,0:T(4,128)(2,1)}), bf16[6144,3,128]{2,1,0:T(4,128)(2,1)}, u32[]{:S(2)}, u32[]{:S(2)}) async-start(bf16[6144,3,128]{2,1,0:T(4,128)(2,1)} %copy.417), calls=%async_computation.7 | async-start | bytes 12582912 | tf_op jit(solution)/shard_map/all_to_all | solution.py:331
  1559.6 40.2 %reduce-scatter.37.cloned.1.call-start = ((), (), s32[]{:S(2)}) async-start(), calls=%async_computation.30 | async-start | bytes 147456
  1566.5 58.6 %reduce-scatter.31.cloned.1.call-start = ((), (), s32[]{:S(2)}) async-start(), calls=%async_computation.25 | async-start | bytes 442368 | tf_op jit(solution)/shard_map/reduce_scatter | solution.py:144
  1574.4 81.7 %reduce-scatter.29.cloned.1.call-start = ((), (), s32[]{:S(2)}) async-start(), calls=%async_computation.24 | async-start | bytes 442368 | tf_op jit(solution)/shard_map/reduce_scatter | solution.py:144
  (111 other events, 495.5 us)
Sparse Core Ops, SparseCore 0:
  15.0 71.2 all-gather.10
  169.8 70.1 all-gather.12
  281.6 70.0 reduce-scatter.20
  357.1 70.3 all-gather.14
  513.4 110.5 all-gather.16
  717.0 70.9 reduce-scatter.24
  791.0 70.1 reduce-scatter.22
  1051.8 64.6 all-gather.18
  1281.5 70.9 reduce-scatter.26
  1354.2 43.3 all-gather.20
  1399.8 27.3 reduce-scatter.42
  1429.9 28.2 reduce-scatter.38
  1460.5 29.0 reduce-scatter.40
  1491.8 29.1 reduce-scatter.34
  1523.1 29.0 reduce-scatter.32
  1566.5 27.5 reduce-scatter.36
  1596.3 28.7 reduce-scatter.30
  1627.3 28.7 reduce-scatter.28
